TPU v7x, 512 devices: a whole 4x8x8 slice. The times are simulated.
512 devices in a mesh: dp: 64 (over z, x, core), class: 8 (over y).
Axes of the slice: x: 4, y: 8, z: 8, core: 2. Of those that a mesh axis runs over, the one named last changes fastest.
Arguments:
- embeddings: bfloat16 [16384, 1024], P('dp', 'class'), may hold values from -28 to 28, as said below
- labels: bfloat16 [16384, 4096], P('dp', 'class'), may hold values from -55 to 55
- head_weight: bfloat16 [1024, 4096], P(None, 'class'), may hold values from -0.1875 to 0.1875
- send_blocks: int32 [64, 64], P('dp'), may hold values from 0 to 1
- nbr_source: int32 [16384, 32], P('dp'), may hold values from 0 to 63
- nbr_offset: int32 [16384, 32], P('dp'), may hold values from 0 to 127
- counts: int32 [16384], P('dp'), may hold values from 1 to 32
Outputs:
- target_logits: bfloat16 [16384, 4096], P('dp', 'class')
- head_grad: bfloat16 [1024, 4096], P(None, 'class')
Inputs may be any that keep to these rules, and one draw needn't show every extreme that they name: Each image of the embeddings has entries within the range. `send_blocks`: entry [p, q] names which of dp index p's own 2 blocks dp index q receives from p. The neighbour lies in the block that this dp index receives from dp index nbr_source. Only the first counts[r] neighbours of image r are used.
All inputs are finite; a program needn't handle non-finite values.
Results may differ from a plain program's by a relative error of at most 0.0062.
Values may be sent and summed in bfloat16 or wider, within the bound.
A program may use at most 64 MiB of HBM per device.

v0:
```python
import math
import jax
import jax.numpy as jnp
from jax import lax
from jax.sharding import PartitionSpec as P

D = 1024
C = 4096
BLOCK = 128


def _combine_stats(local_max, local_sum):
    both = lax.all_gather(jnp.stack([local_max, local_sum], axis=0), "class", axis=0)
    maxes, sums = (both[:, 0], both[:, 1])
    top = jnp.max(maxes, axis=0)
    total = jnp.sum(sums * jnp.exp(maxes - top[None, :]), axis=0)
    return (top, total)


def on_device(embeddings, labels, head_weight, send_blocks, nbr_source, nbr_offset, counts):
    rows = embeddings.shape[0]
    width_part = embeddings.shape[1]
    class_part = labels.shape[1]
    dp_count = lax.axis_size("dp")
    nbrs = nbr_source.shape[1]
    picks = send_blocks[0]
    out_emb = embeddings.reshape(rows // BLOCK, BLOCK, width_part)[picks]
    out_lab = labels.reshape(rows // BLOCK, BLOCK, class_part)[picks]
    pool_emb = lax.all_to_all(out_emb, "dp", split_axis=0, concat_axis=0, tiled=True)
    pool_lab = lax.all_to_all(out_lab, "dp", split_axis=0, concat_axis=0, tiled=True)
    pool_rows = dp_count * BLOCK
    pool_emb = pool_emb.reshape(pool_rows, width_part)
    pool_lab = pool_lab.reshape(pool_rows, class_part)
    located = nbr_source * BLOCK + nbr_offset
    full_emb = lax.all_gather(embeddings, "class", axis=1, tiled=True)
    head = jnp.dot(full_emb, head_weight, preferred_element_type=jnp.float32)
    h_top, h_total = _combine_stats(
        jnp.max(head, axis=1), jnp.sum(jnp.exp(head - jnp.max(head, axis=1, keepdims=True)), axis=1)
    )
    prob_head = jnp.exp(head - h_top[:, None]) / h_total[:, None]
    near = pool_emb[located]
    partial_value = jnp.einsum("rd,rkd->rk", embeddings, near, preferred_element_type=jnp.float32)
    scores = lax.psum(partial_value, "class")
    valid = lax.broadcasted_iota(jnp.int32, (rows, nbrs), 1) < counts[:, None]
    logits = jnp.where(valid, scores / math.sqrt(D), -1e30)
    top = jnp.max(logits, axis=1, keepdims=True)
    expd = jnp.where(valid, jnp.exp(logits - top), 0.0)
    weights = (expd / jnp.sum(expd, axis=1, keepdims=True)).astype(jnp.bfloat16)
    row_ids = lax.broadcasted_iota(jnp.int32, (rows, nbrs), 0)
    dense = (
        jnp.zeros((rows, pool_rows), jnp.float32)
        .at[row_ids, located]
        .add(weights.astype(jnp.float32))
    )
    dense_hi = dense.astype(jnp.bfloat16)
    dense_lo = (dense - dense_hi.astype(jnp.float32)).astype(jnp.bfloat16)
    spread = jnp.dot(dense_hi, pool_lab, preferred_element_type=jnp.float32) + jnp.dot(
        dense_lo, pool_lab, preferred_element_type=jnp.float32
    )
    target = 4.0 * spread + labels.astype(jnp.float32)
    z_local = jnp.max(target, axis=1)
    z_top, z_total = _combine_stats(z_local, jnp.sum(jnp.exp(target - z_local[:, None]), axis=1))
    prob_target = jnp.exp(target - z_top[:, None]) / z_total[:, None]
    diff = (C * (prob_head - prob_target)).astype(jnp.bfloat16)
    part_grad = lax.dot_general(
        full_emb, diff, (((0,), (0,)), ((), ())), preferred_element_type=jnp.float32
    )
    scale = 1.0 / math.sqrt(rows * dp_count)
    limit = 0.5 * math.sqrt(D * C)
    summed = lax.psum_scatter(part_grad, "dp", scatter_dimension=0, tiled=True) * scale
    squared = lax.psum(jnp.sum(summed * summed), ("dp", "class"))
    factor = jnp.minimum(1.0, limit / jnp.sqrt(squared))
    head_grad = lax.all_gather((summed * factor).astype(jnp.bfloat16), "dp", axis=0, tiled=True)
    return (target.astype(jnp.bfloat16), head_grad)


def solution(mesh):
    return jax.shard_map(
        on_device,
        mesh=mesh,
        in_specs=(
            P("dp", "class"),
            P("dp", "class"),
            P(None, "class"),
            P("dp", None),
            P("dp", None),
            P("dp", None),
            P("dp"),
        ),
        out_specs=(P("dp", "class"), P(None, "class")),
        check_vma=False,
    )
```

profile of v0, /device:TPU:1, one launch (start us, length us, event | category | flops | bytes accessed | tf_op | source)
XLA Modules:
  0.0 644.6 jit_solution(2418893639809104688)
XLA Ops:
  7.2 0.0 copy-start
  7.2 0.8 fusion.31
  8.0 3.0 gather_fusion
  11.0 14.8 %all-to-all-start = ((bf16[64,128,128]{2,1,0:T(8,128)(2,1)}), bf16[64,128,128]{2,1,0:T(8,128)(2,1)S(1)}, u32[]{:S(2)}, u32[]{:S(2)}) async-start(bf16[64,128,128]{2,1,0:T(8,128)(2,1)} %gather_fusion), calls=%async_computation | async-start | bytes 4194304 | tf_op jit(solution)/shard_map/all_to_all | solution.py:29
  25.8 5.4 gather_fusion.2
  31.2 44.3 %all-to-all-done = bf16[64,128,128]{2,1,0:T(8,128)(2,1)S(1)} async-done(((bf16[64,128,128]{2,1,0:T(8,128)(2,1)}), bf16[64,128,128]{2,1,0:T(8,128)(2,1)S(1)}, u32[]{:S(2)}, u32[]{:S(2)}) %all-to-all-start) | async-done | bytes 2097184 | tf_op jit(solution)/shard_map/all_to_all | solution.py:29
  75.5 7.2 %all-to-all-start.1 = ((bf16[64,128,512]{2,1,0:T(8,128)(2,1)}), bf16[64,128,512]{2,1,0:T(8,128)(2,1)}, u32[]{:S(2)}, u32[]{:S(2)}) async-start(bf16[64,128,512]{2,1,0:T(8,128)(2,1)} %gather_fusion.2), calls=%async_computation.1 | async-start | bytes 16777216 | tf_op jit(solution)/shard_map/all_to_all | solution.py:30
  82.7 0.0 reduce-scatter.4.cloned.1.call-start
  82.8 0.8 compare_select_fusion
  83.6 0.8 copy.22
  84.3 0.1 multiply_reduce_fusion.1
  84.4 0.1 and_reduce_fusion
  84.5 0.8 copy.21
  85.3 1.6 reshape.99
  86.9 1.0 reshape.85
  87.9 22.7 %all_gather.18 = bf16[256,1024]{1,0:T(8,128)(2,1)S(1)} all-gather(bf16[256,128]{1,0:T(8,128)(2,1)S(1)} %copy-done.2), channel_id=1, replica_groups=mesh['dp'=64,'class'=8] {'class'}, dimensions={1}, use_global_device_ids=true | all-gather | bytes 589824 | tf_op jit(solution)/shard_map/all_gather | solution.py:35
  110.6 0.8 copy-done.4
  111.4 0.5 fusion.34
  111.9 0.8 copy-done.6
  112.7 0.2 exponential_reduce_fusion.1
  112.9 18.0 %all-gather.2 = f32[8,2,256]{2,1,0:T(2,128)S(1)} all-gather(f32[1,2,256]{2,1,0:T(2,128)S(1)} %maximum_bitcast_fusion), channel_id=2, replica_groups=mesh['dp'=64,'class'=8] {'class'}, dimensions={0}, use_global_device_ids=true | all-gather | bytes 18432 | tf_op jit(solution)/shard_map/all_gather | solution.py:13
  131.0 0.0 copy-start.9
  131.0 29.2 %gather_fusion.1 = bf16[8192,128]{1,0:T(8,128)(2,1)} fusion(bf16[8192,128]{1,0:T(8,128)(2,1)S(1)} %bitcast.55, s32[8192]{0:T(1024)S(1)} %broadcast_clamp_fusion), kind=kCustom, calls=%fused_computation.1 | custom fusion | bytes 4227072 | tf_op jit(solution)/shard_map/gather | solution.py:41
  160.2 2.8 fusion.20
  163.0 24.4 %psum.14 = f32[256,32]{1,0:T(8,128)S(1)} all-reduce(f32[256,32]{1,0:T(8,128)S(1)} %bitcast.61), channel_id=1, replica_groups=mesh['dp'=64,'class'=8] {'class'}, use_global_device_ids=true, to_apply=%region_0.0 | all-reduce | flops 8192 | bytes 65536 | tf_op jit(solution)/shard_map/psum | solution.py:43
  187.4 0.2 fusion.22
  187.6 0.2 fusion.23
  187.8 0.2 fusion.24
  188.0 0.1 reshape.101
  188.1 47.1 %scatter_custom_fusion = f32[2097152]{0:T(1024)} fusion(s32[8192]{0:T(1024)} %reshape.99, f32[8192]{0:T(1024)S(1)} %reshape.101, f32[]{:T(128)} %constant.13.clone.1), kind=kCustom, calls=%fused_computation.6 | custom fusion | flops 8192 | bytes 8389120
  235.2 9.4 %reshape.74 = f32[256,8192]{1,0:T(8,128)} reshape(f32[2097152]{0:T(1024)} %scatter_custom_fusion) | data formatting | bytes 16777216 | tf_op jit(solution)/shard_map/scatter-add | solution.py:53
  244.6 21.0 %all-to-all-done.1 = bf16[64,128,512]{2,1,0:T(8,128)(2,1)} async-done(((bf16[64,128,512]{2,1,0:T(8,128)(2,1)}), bf16[64,128,512]{2,1,0:T(8,128)(2,1)}, u32[]{:S(2)}, u32[]{:S(2)}) %all-to-all-start.1) | async-done | bytes 8388640 | tf_op jit(solution)/shard_map/all_to_all | solution.py:30
  265.6 10.6 %fusion = f32[256,512]{1,0:T(8,128)S(1)} fusion(bf16[8192,512]{1,0:T(8,128)(2,1)} %bitcast.10, f32[256,8192]{1,0:T(8,128)} %reshape.74), kind=kOutput, calls=%fused_computation.5 | convolution fusion | flops 2155872256 | bytes 17301504 | tf_op jit(solution)/shard_map/dot_general | solution.py:57
  276.3 5.9 fusion.33
  282.2 0.9 exponential_reduce_fusion
  283.1 18.3 %all-gather.3 = f32[8,2,256]{2,1,0:T(2,128)S(1)} all-gather(f32[1,2,256]{2,1,0:T(2,128)S(1)} %maximum_bitcast_fusion.1), channel_id=3, replica_groups=mesh['dp'=64,'class'=8] {'class'}, dimensions={0}, use_global_device_ids=true | all-gather | bytes 18432 | tf_op jit(solution)/shard_map/all_gather | solution.py:13
  301.4 0.7 convolution_bitcast_fusion
  302.1 1.9 copy.28
  304.0 0.0 reduce-scatter.4.cloned.1.call-update
  304.0 0.0 all-gather.6.cloned.1.call-start
  304.1 147.5 %reduce-scatter.4.cloned.1.call-done = f32[16,512]{1,0:T(8,128)} async-done(((f32[1024,512]{1,0:T(8,128)}), f32[16,512]{1,0:T(8,128)}) %reduce-scatter.4.cloned.1.call-update) | async-done | bytes 32784 | tf_op jit(solution)/shard_map/reduce_scatter | solution.py:70
  451.6 0.9 copy.29
  452.5 0.7 multiply_reduce_fusion
  453.2 100.5 %psum.15 = f32[]{:T(128)} all-reduce(f32[]{:T(128)} %multiply_reduce_fusion), channel_id=1, replica_groups=mesh['dp'=64,'class'=8] {'dp','class'}, use_global_device_ids=true, to_apply=%region_14.15 | all-reduce | flops 1 | bytes 8 | tf_op jit(solution)/shard_map/psum | solution.py:71
  554.3 1.4 multiply_convert_fusion.2
  555.7 0.0 all-gather.6.cloned.1.call-update
  555.7 79.7 %all-gather.6.cloned.1.call-done = bf16[1024,512]{1,0:T(8,128)(2,1)} async-done(((bf16[16,512]{1,0:T(8,128)(2,1)}), bf16[1024,512]{1,0:T(8,128)(2,1)}) %all-gather.6.cloned.1.call-update) | async-done | bytes 1048592 | tf_op jit(solution)/shard_map/all_gather | solution.py:73
  635.5 2.3 copy.49
  (30 shorter events, 0.2 us)
Async XLA Ops:
  7.2 104.2 %copy-start = (bf16[1024,512]{1,0:T(8,128)(2,1)S(1)}, bf16[1024,512]{1,0:T(8,128)(2,1)}, u32[]{:S(2)}) copy-start(bf16[1024,512]{1,0:T(8,128)(2,1)} %param.9) | copy-start | bytes 3145732
  7.2 18.6 %copy-start.1 = (bf16[256,512]{1,0:T(8,128)(2,1)S(1)}, bf16[256,512]{1,0:T(8,128)(2,1)}, u32[]{:S(2)}) copy-start(bf16[256,512]{1,0:T(8,128)(2,1)} %param.8) | copy-start | bytes 786436
  11.0 64.5 %all-to-all-start = ((bf16[64,128,128]{2,1,0:T(8,128)(2,1)}), bf16[64,128,128]{2,1,0:T(8,128)(2,1)S(1)}, u32[]{:S(2)}, u32[]{:S(2)}) async-start(bf16[64,128,128]{2,1,0:T(8,128)(2,1)} %gather_fusion), calls=%async_computation | async-start | bytes 4194304 | tf_op jit(solution)/shard_map/all_to_all | solution.py:29
  31.2 51.6 %copy-start.8 = (s32[256,32]{0,1:T(8,128)S(1)}, s32[256,32]{0,1:T(8,128)}, u32[]{:S(2)}) copy-start(s32[256,32]{0,1:T(8,128)} %param.12) | copy-start | bytes 98308
  31.2 53.2 %copy-start.10 = (s32[2]{0:T(128)S(1)}, s32[2]{0:T(128)}, u32[]{:S(2)}) copy-start(s32[2]{0:T(128)} %constant.33) | copy-start | bytes 28
  31.2 53.2 %copy-start.11 = (s32[2]{0:T(128)S(1)}, s32[2]{0:T(128)}, u32[]{:S(2)}) copy-start(s32[2]{0:T(128)} %constant.36) | copy-start | bytes 28
  31.2 56.7 %copy-start.2 = (bf16[256,128]{1,0:T(8,128)(2,1)S(1)}, bf16[256,128]{1,0:T(8,128)(2,1)}, u32[]{:S(2)}) copy-start(bf16[256,128]{1,0:T(8,128)(2,1)} %param.7) | copy-start | bytes 196612
  75.5 190.1 %all-to-all-start.1 = ((bf16[64,128,512]{2,1,0:T(8,128)(2,1)}), bf16[64,128,512]{2,1,0:T(8,128)(2,1)}, u32[]{:S(2)}, u32[]{:S(2)}) async-start(bf16[64,128,512]{2,1,0:T(8,128)(2,1)} %gather_fusion.2), calls=%async_computation.1 | async-start | bytes 16777216 | tf_op jit(solution)/shard_map/all_to_all | solution.py:30
  82.7 368.9 %reduce-scatter.4.cloned.1.call-start = ((), (), s32[]{:S(2)}) async-start(), calls=%async_computation.4 | async-start | bytes 2129920 | tf_op jit(solution)/shard_map/reduce_scatter | solution.py:70
  110.6 0.8 copy-start.4
  111.9 0.8 copy-start.6
  131.0 56.4 %copy-start.9 = (s32[256]{0:T(256)S(1)}, s32[256]{0:T(256)}, u32[]{:S(2)}) copy-start(s32[256]{0:T(256)} %param.13) | copy-start | bytes 3076
  265.6 10.6 %copy-start.3 = (f32[256,8192]{1,0:T(8,128)S(1)}, f32[256,8192]{1,0:T(8,128)}, u32[]{:S(2)}) copy-start(f32[256,8192]{1,0:T(8,128)} %reshape.74) | copy-start | bytes 25165828
  276.3 25.1 %copy-start.5 = (bf16[256,1024]{1,0:T(8,128)(2,1)S(1)}, bf16[256,1024]{1,0:T(8,128)(2,1)}, u32[]{:S(2)}) copy-start(bf16[256,1024]{1,0:T(8,128)(2,1)} %copy-done.4) | copy-start | bytes 1572868
  276.3 25.1 %copy-start.7 = (f32[256,512]{1,0:T(8,128)S(1)}, f32[256,512]{1,0:T(8,128)}, u32[]{:S(2)}) copy-start(f32[256,512]{1,0:T(8,128)} %copy-done.6) | copy-start | bytes 1572868
  304.0 331.4 %all-gather.6.cloned.1.call-start = ((), (), s32[]{:S(2)}) async-start(), calls=%async_computation.3 | async-start | bytes 1064960 | tf_op jit(solution)/shard_map/all_gather | solution.py:73
Sparse Core Ops, SparseCore 0:
  304.2 147.3 reduce-scatter.3
  555.8 79.5 all-gather.5
where the time goes:
time: 645 us
  waiting for transfers between devices  293 us (45%)
  blocking collectives  184 us (29%)
  local copies, waits for them, and re-layouts  57.8 us (9%)
  other arithmetic  52.6 us (8%)
  starting transfers between devices  22.2 us (3%)
  matrix products  20.5 us (3%)
  between operations  15 us (2%)
    reduce_scatter x1, waiting for transfers between devices, on_device(): lax.psum_scatter(part_grad, 'dp', scatter_dimension=0, tiled=True) * scale  148 us
    psum x1, blocking collectives, on_device(): squared = lax.psum(jnp.sum(summed * summed), ('dp', 'class'))  100 us
    all_gather x1, waiting for transfers between devices, on_device(): lax.all_gather((summed * factor).astype(jnp.bfloat16), 'dp', axis=0, tile...  79.7 us
    unnamed x6, other arithmetic  47.3 us
    all_to_all x1, waiting for transfers between devices, on_device(): lax.all_to_all(out_emb, 'dp', split_axis=0, concat_axis=0, tiled=True)  44.3 us
    all_gather x2, blocking collectives, _combine_stats(): lax.all_gather(jnp.stack([local_max, local_sum], axis=0), 'class', axis=0)  36.2 us
    gather x1, local copies, waits for them, and re-layouts, on_device(): near = pool_emb[located]  29.2 us
    psum x1, blocking collectives, on_device(): scores = lax.psum(partial_value, 'class')  24.4 us
  transfers between devices with their start and end apart: 4, of which 4 were waited for; matrix products, arithmetic and copies ran while one was open for 16% of the time, Pallas kernels for 0%

commit v1 on v0

--- a/solution.py
+++ b/solution.py
@@ -32,7 +32,9 @@
     pool_emb = pool_emb.reshape(pool_rows, width_part)
     pool_lab = pool_lab.reshape(pool_rows, class_part)
     located = nbr_source * BLOCK + nbr_offset
-    full_emb = lax.all_gather(embeddings, "class", axis=1, tiled=True)
+    full_emb = jnp.concatenate(
+        lax.all_to_all(jnp.stack([embeddings] * lax.axis_size("class")), "class", 0, 0), axis=1
+    )
     head = jnp.dot(full_emb, head_weight, preferred_element_type=jnp.float32)
     h_top, h_total = _combine_stats(
         jnp.max(head, axis=1), jnp.sum(jnp.exp(head - jnp.max(head, axis=1, keepdims=True)), axis=1)

time: 645 us -> 667 us (1.034)
  waiting for transfers between devices: 293 us -> 328 us
  blocking collectives: 184 us -> 159 us
  starting transfers between devices: 22.2 us -> 32 us
    all_to_all x1, waiting for transfers between devices: 21 us -> 45 us  [on_device(): lax.all_to_all(out_lab, 'dp', split_axis=0, concat_axis=0, tiled=True)]
    all_gather x1 -> x0, blocking collectives: 22.7 us -> none  [on_device(): full_emb = lax.all_gather(embeddings, 'class', axis=1, tiled=True)]
    all_to_all x0 -> x1, waiting for transfers between devices: none -> 11.1 us  [on_device(): lax.all_to_all(jnp.stack([embeddings] * lax.axis_size('class')), 'class',...]
    all_to_all x0 -> x1, starting transfers between devices: none -> 7.65 us  [on_device(): lax.all_to_all(jnp.stack([embeddings] * lax.axis_size('class')), 'class',...]
  transfers between devices with their start and end apart: 4 -> 5, of which waited for: 4 -> 5; matrix products, arithmetic and copies ran while one was open for 16% -> 16% of each run, Pallas kernels for 0% -> 0%
where the time goes in v1:
time: 667 us; the launch traced here: 666 us
  waiting for transfers between devices  328 us (49%)
  blocking collectives  159 us (24%)
  local copies, waits for them, and re-layouts  58.1 us (9%)
  other arithmetic  52.4 us (8%)
  starting transfers between devices  32 us (5%)
  matrix products  21.6 us (3%)
  between operations  15 us (2%)
    reduce_scatter x1, waiting for transfers between devices, on_device(): lax.psum_scatter(part_grad, 'dp', scatter_dimension=0, tiled=True) * scale  148 us
    psum x1, blocking collectives, on_device(): squared = lax.psum(jnp.sum(summed * summed), ('dp', 'class'))  101 us
    all_gather x1, waiting for transfers between devices, on_device(): lax.all_gather((summed * factor).astype(jnp.bfloat16), 'dp', axis=0, tile...  79.7 us
    unnamed x6, other arithmetic  47.9 us
    all_to_all x1, waiting for transfers between devices, on_device(): lax.all_to_all(out_lab, 'dp', split_axis=0, concat_axis=0, tiled=True)  45 us
    all_to_all x1, waiting for transfers between devices, on_device(): lax.all_to_all(out_emb, 'dp', split_axis=0, concat_axis=0, tiled=True)  44.3 us
    all_gather x2, blocking collectives, _combine_stats(): lax.all_gather(jnp.stack([local_max, local_sum], axis=0), 'class', axis=0)  33.5 us
    gather x1, local copies, waits for them, and re-layouts, on_device(): near = pool_emb[located]  29.2 us
  transfers between devices with their start and end apart: 5, of which 5 were waited for; matrix products, arithmetic and copies ran while one was open for 16% of the time, Pallas kernels for 0%

profile of v1, /device:TPU:1, one launch (start us, length us, event | category | flops | bytes accessed | tf_op | source)
XLA Modules:
  0.0 665.5 jit_solution(3290719772116988344)
XLA Ops:
  7.2 1.0 copy.25
  8.2 0.8 stack.14
  9.1 7.7 %all-to-all-start.2 = ((bf16[8,256,128]{1,2,0:T(8,128)(2,1)}), bf16[8,256,128]{1,2,0:T(8,128)(2,1)S(1)}, u32[]{:S(2)}, u32[]{:S(2)}) async-start(bf16[8,256,128]{1,2,0:T(8,128)(2,1)} %stack.14), calls=%async_computation.2 | async-start | bytes 1048576 | tf_op jit(solution)/shard_map/all_to_all | solution.py:36
  16.7 0.7 fusion.31
  17.4 3.0 gather_fusion
  20.4 11.1 %all-to-all-done.2 = bf16[8,256,128]{1,2,0:T(8,128)(2,1)S(1)} async-done(((bf16[8,256,128]{1,2,0:T(8,128)(2,1)}), bf16[8,256,128]{1,2,0:T(8,128)(2,1)S(1)}, u32[]{:S(2)}, u32[]{:S(2)}) %all-to-all-start.2) | async-done | bytes 524320 | tf_op jit(solution)/shard_map/all_to_all | solution.py:36
  31.5 0.8 copy-done.4
  32.3 17.0 %all-to-all-start = ((bf16[64,128,128]{2,1,0:T(8,128)(2,1)}), bf16[64,128,128]{2,1,0:T(8,128)(2,1)S(1)}, u32[]{:S(2)}, u32[]{:S(2)}) async-start(bf16[64,128,128]{2,1,0:T(8,128)(2,1)} %gather_fusion), calls=%async_computation | async-start | bytes 4194304 | tf_op jit(solution)/shard_map/all_to_all | solution.py:29
  49.3 5.4 gather_fusion.2
  54.7 44.3 %all-to-all-done = bf16[64,128,128]{2,1,0:T(8,128)(2,1)S(1)} async-done(((bf16[64,128,128]{2,1,0:T(8,128)(2,1)}), bf16[64,128,128]{2,1,0:T(8,128)(2,1)S(1)}, u32[]{:S(2)}, u32[]{:S(2)}) %all-to-all-start) | async-done | bytes 2097184 | tf_op jit(solution)/shard_map/all_to_all | solution.py:29
  99.0 7.2 %all-to-all-start.1 = ((bf16[64,128,512]{2,1,0:T(8,128)(2,1)}), bf16[64,128,512]{2,1,0:T(8,128)(2,1)}, u32[]{:S(2)}, u32[]{:S(2)}) async-start(bf16[64,128,512]{2,1,0:T(8,128)(2,1)} %gather_fusion.2), calls=%async_computation.1 | async-start | bytes 16777216 | tf_op jit(solution)/shard_map/all_to_all | solution.py:30
  106.2 0.0 reduce-scatter.4.cloned.1.call-start
  106.3 0.8 copy.24
  107.1 0.1 multiply_reduce_fusion.1
  107.2 0.1 and_reduce_fusion
  107.2 0.6 broadcast_select_fusion
  107.9 0.9 copy.23
  108.7 0.7 reshape.109
  109.4 1.0 reshape.95
  110.4 1.6 fusion.34
  112.0 0.2 exponential_reduce_fusion.1
  112.2 18.0 %all-gather.2 = f32[8,2,256]{2,1,0:T(2,128)S(1)} all-gather(f32[1,2,256]{2,1,0:T(2,128)S(1)} %maximum_bitcast_fusion), channel_id=2, replica_groups=mesh['dp'=64,'class'=8] {'class'}, dimensions={0}, use_global_device_ids=true | all-gather | bytes 18432 | tf_op jit(solution)/shard_map/all_gather | solution.py:13
  130.3 29.2 %gather_fusion.1 = bf16[8192,128]{1,0:T(8,128)(2,1)} fusion(bf16[8192,128]{1,0:T(8,128)(2,1)S(1)} %bitcast.58, s32[8192]{0:T(1024)S(1)} %broadcast_clamp_fusion), kind=kCustom, calls=%fused_computation.1 | custom fusion | bytes 4227072 | tf_op jit(solution)/shard_map/gather | solution.py:43
  159.6 2.8 fusion.20
  162.3 24.6 %psum.14 = f32[256,32]{1,0:T(8,128)S(1)} all-reduce(f32[256,32]{1,0:T(8,128)S(1)} %bitcast.66), channel_id=1, replica_groups=mesh['dp'=64,'class'=8] {'class'}, use_global_device_ids=true, to_apply=%region_0.0 | all-reduce | flops 8192 | bytes 65536 | tf_op jit(solution)/shard_map/psum | solution.py:45
  186.9 0.2 fusion.22
  187.1 0.2 fusion.23
  187.3 0.2 fusion.24
  187.5 0.1 reshape.111
  187.6 47.1 %scatter_custom_fusion = f32[2097152]{0:T(1024)} fusion(s32[8192]{0:T(1024)} %reshape.109, f32[8192]{0:T(1024)S(1)} %reshape.111, f32[]{:T(128)} %constant.13.clone.1), kind=kCustom, calls=%fused_computation.6 | custom fusion | flops 8192 | bytes 8389120
  234.7 9.4 %reshape.84 = f32[256,8192]{1,0:T(8,128)} reshape(f32[2097152]{0:T(1024)} %scatter_custom_fusion) | data formatting | bytes 16777216 | tf_op jit(solution)/shard_map/scatter-add | solution.py:55
  244.1 45.0 %all-to-all-done.1 = bf16[64,128,512]{2,1,0:T(8,128)(2,1)} async-done(((bf16[64,128,512]{2,1,0:T(8,128)(2,1)}), bf16[64,128,512]{2,1,0:T(8,128)(2,1)}, u32[]{:S(2)}, u32[]{:S(2)}) %all-to-all-start.1) | async-done | bytes 8388640 | tf_op jit(solution)/shard_map/all_to_all | solution.py:30
  289.1 10.6 %fusion = f32[256,512]{1,0:T(8,128)S(1)} fusion(bf16[8192,512]{1,0:T(8,128)(2,1)} %bitcast.10, f32[256,8192]{1,0:T(8,128)} %reshape.84), kind=kOutput, calls=%fused_computation.5 | convolution fusion | flops 2155872256 | bytes 17301504 | tf_op jit(solution)/shard_map/dot_general | solution.py:59
  299.8 5.9 fusion.33
  305.7 0.9 exponential_reduce_fusion
  306.5 15.4 %all-gather.3 = f32[8,2,256]{2,1,0:T(2,128)S(1)} all-gather(f32[1,2,256]{2,1,0:T(2,128)S(1)} %maximum_bitcast_fusion.1), channel_id=3, replica_groups=mesh['dp'=64,'class'=8] {'class'}, dimensions={0}, use_global_device_ids=true | all-gather | bytes 18432 | tf_op jit(solution)/shard_map/all_gather | solution.py:13
  322.1 0.8 convolution_bitcast_fusion
  322.8 1.9 copy.31
  324.7 0.0 reduce-scatter.4.cloned.1.call-update
  324.7 0.0 all-gather.6.cloned.1.call-start
  324.8 147.8 %reduce-scatter.4.cloned.1.call-done = f32[16,512]{1,0:T(8,128)} async-done(((f32[1024,512]{1,0:T(8,128)}), f32[16,512]{1,0:T(8,128)}) %reduce-scatter.4.cloned.1.call-update) | async-done | bytes 32784 | tf_op jit(solution)/shard_map/reduce_scatter | solution.py:72
  472.5 0.9 copy.32
  473.4 0.7 multiply_reduce_fusion
  474.1 100.5 %psum.15 = f32[]{:T(128)} all-reduce(f32[]{:T(128)} %multiply_reduce_fusion), channel_id=1, replica_groups=mesh['dp'=64,'class'=8] {'dp','class'}, use_global_device_ids=true, to_apply=%region_14.15 | all-reduce | flops 1 | bytes 8 | tf_op jit(solution)/shard_map/psum | solution.py:73
  575.3 1.4 multiply_convert_fusion.2
  576.7 0.0 all-gather.6.cloned.1.call-update
  576.7 79.7 %all-gather.6.cloned.1.call-done = bf16[1024,512]{1,0:T(8,128)(2,1)} async-done(((bf16[16,512]{1,0:T(8,128)(2,1)}), bf16[1024,512]{1,0:T(8,128)(2,1)}) %all-gather.6.cloned.1.call-update) | async-done | bytes 1048592 | tf_op jit(solution)/shard_map/all_gather | solution.py:75
  656.4 2.3 copy.52
  (35 shorter events, 0.2 us)
Async XLA Ops:
  7.2 103.3 %copy-start = (bf16[1024,512]{1,0:T(8,128)(2,1)S(1)}, bf16[1024,512]{1,0:T(8,128)(2,1)}, u32[]{:S(2)}) copy-start(bf16[1024,512]{1,0:T(8,128)(2,1)} %param.9) | copy-start | bytes 3145732
  7.2 42.1 %copy-start.1 = (bf16[256,512]{1,0:T(8,128)(2,1)S(1)}, bf16[256,512]{1,0:T(8,128)(2,1)}, u32[]{:S(2)}) copy-start(bf16[256,512]{1,0:T(8,128)(2,1)} %param.8) | copy-start | bytes 786436
  9.1 22.4 %all-to-all-start.2 = ((bf16[8,256,128]{1,2,0:T(8,128)(2,1)}), bf16[8,256,128]{1,2,0:T(8,128)(2,1)S(1)}, u32[]{:S(2)}, u32[]{:S(2)}) async-start(bf16[8,256,128]{1,2,0:T(8,128)(2,1)} %stack.14), calls=%async_computation.2 | async-start | bytes 1048576 | tf_op jit(solution)/shard_map/all_to_all | solution.py:36
  31.5 0.8 copy-start.4
  32.3 66.7 %all-to-all-start = ((bf16[64,128,128]{2,1,0:T(8,128)(2,1)}), bf16[64,128,128]{2,1,0:T(8,128)(2,1)S(1)}, u32[]{:S(2)}, u32[]{:S(2)}) async-start(bf16[64,128,128]{2,1,0:T(8,128)(2,1)} %gather_fusion), calls=%async_computation | async-start | bytes 4194304 | tf_op jit(solution)/shard_map/all_to_all | solution.py:29
  54.7 51.6 %copy-start.8 = (s32[256,32]{0,1:T(8,128)S(1)}, s32[256,32]{0,1:T(8,128)}, u32[]{:S(2)}) copy-start(s32[256,32]{0,1:T(8,128)} %param.12) | copy-start | bytes 98308
  54.7 51.6 %copy-start.9 = (s32[256,32]{0,1:T(8,128)S(1)}, s32[256,32]{0,1:T(8,128)}, u32[]{:S(2)}) copy-start(s32[256,32]{0,1:T(8,128)} %param.11) | copy-start | bytes 98308
  54.7 52.4 %copy-start.11 = (s32[2]{0:T(128)S(1)}, s32[2]{0:T(128)}, u32[]{:S(2)}) copy-start(s32[2]{0:T(128)} %constant.33) | copy-start | bytes 28
  54.7 52.5 %copy-start.12 = (s32[2]{0:T(128)S(1)}, s32[2]{0:T(128)}, u32[]{:S(2)}) copy-start(s32[2]{0:T(128)} %constant.36) | copy-start | bytes 28
  99.0 190.1 %all-to-all-start.1 = ((bf16[64,128,512]{2,1,0:T(8,128)(2,1)}), bf16[64,128,512]{2,1,0:T(8,128)(2,1)}, u32[]{:S(2)}, u32[]{:S(2)}) async-start(bf16[64,128,512]{2,1,0:T(8,128)(2,1)} %gather_fusion.2), calls=%async_computation.1 | async-start | bytes 16777216 | tf_op jit(solution)/shard_map/all_to_all | solution.py:30
  106.2 366.3 %reduce-scatter.4.cloned.1.call-start = ((), (), s32[]{:S(2)}) async-start(), calls=%async_computation.5 | async-start | bytes 2129920 | tf_op jit(solution)/shard_map/reduce_scatter | solution.py:72
  112.0 18.3 %copy-start.6 = (f32[256,512]{1,0:T(8,128)}, f32[256,512]{1,0:T(8,128)S(1)}, u32[]{:S(2)}) copy-start(f32[256,512]{1,0:T(8,128)S(1)} %get-tuple-element.17) | copy-start | bytes 1572868
  130.3 29.2 %copy-start.2 = (bf16[256,128]{1,0:T(8,128)(2,1)S(1)}, bf16[256,128]{1,0:T(8,128)(2,1)}, u32[]{:S(2)}) copy-start(bf16[256,128]{1,0:T(8,128)(2,1)} %param.7) | copy-start | bytes 196612
  130.3 56.6 %copy-start.10 = (s32[256]{0:T(256)S(1)}, s32[256]{0:T(256)}, u32[]{:S(2)}) copy-start(s32[256]{0:T(256)} %param.13) | copy-start | bytes 3076
  289.1 10.6 %copy-start.3 = (f32[256,8192]{1,0:T(8,128)S(1)}, f32[256,8192]{1,0:T(8,128)}, u32[]{:S(2)}) copy-start(f32[256,8192]{1,0:T(8,128)} %reshape.84) | copy-start | bytes 25165828
  299.8 22.3 %copy-start.5 = (bf16[8,256,128]{1,2,0:T(8,128)(2,1)S(1)}, bf16[8,256,128]{1,2,0:T(8,128)(2,1)}, u32[]{:S(2)}) copy-start(bf16[8,256,128]{1,2,0:T(8,128)(2,1)} %copy-done.4) | copy-start | bytes 1572868
  299.8 22.3 %copy-start.7 = (f32[256,512]{1,0:T(8,128)S(1)}, f32[256,512]{1,0:T(8,128)}, u32[]{:S(2)}) copy-start(f32[256,512]{1,0:T(8,128)} %copy-done.6) | copy-start | bytes 1572868
  324.7 331.7 %all-gather.6.cloned.1.call-start = ((), (), s32[]{:S(2)}) async-start(), calls=%async_computation.4 | async-start | bytes 1064960 | tf_op jit(solution)/shard_map/all_gather | solution.py:75
Sparse Core Ops, SparseCore 0:
  324.9 147.6 reduce-scatter.3
  576.8 79.5 all-gather.5
